TPU v7x, 32 devices: a whole 2x2x4 slice. The times are simulated.
32 devices in a mesh: frame: 8 (over y, x, core), pix: 4 (over z).
Axes of the slice: x: 2, y: 2, z: 4, core: 2. Of those that a mesh axis runs over, the one named last changes fastest.
Arguments:
- frames: float32 [2048, 1024], P('frame', 'pix'), may hold values from 0.1 to 10
- roi_ids: int32 [1024, 1], P('pix'), may hold values from 0 to 3; in each aligned block of 256 rows (0 to 255, 256 to 511, ...) at most 96 rows name the same one
- roi_order: int32 [4], replicated, may hold values from 0 to 3, each once
Outputs:
- correlation: float32 [4, 2048, 2048], P('pix', 'frame')
Inputs may be any that keep to these rules, and one draw needn't show every extreme that they name: `roi_ids`: among the 256 pixels of one pix index no q-ROI has more than 96 pixels, and some q-ROI has exactly 96; every q-ROI has at least one pixel. `roi_order`: each q-ROI appears once; owner slot j lies on pix index j.
All inputs are finite; a program needn't handle non-finite values.
Results may differ from a plain program's by a relative error of at most 0.0003.
Values sent between devices are 32-bit elements; how exact they have to be, the bound alone decides.
A program may use at most 64 MiB of HBM per device.

v0:
```python
import jax
import jax.numpy as jnp
from jax import lax
from jax.sharding import PartitionSpec as P

SLOT = 96


def shifted(value, axis, steps):
    count = lax.axis_size(axis)
    pairs = [(source, (source + steps) % count) for source in range(count)]
    return lax.ppermute(value, axis, pairs)


def per_device(frames, roi_ids, roi_order):
    fr_dev, pix_dev = frames.shape
    npix = lax.axis_size("pix")
    nframe = lax.axis_size("frame")
    rois = roi_order.shape[0]
    roi_dev = rois // npix
    slot = SLOT
    ids = roi_ids[:, 0]
    labels = jnp.arange(rois, dtype=jnp.int32)
    onehot = (ids[:, None] == labels[None, :]).astype(jnp.int32)
    rank = jnp.sum(onehot * (jnp.cumsum(onehot, axis=0) - 1), axis=1)
    holder = (roi_order[None, :] == labels[:, None]).astype(jnp.int32)
    position = jnp.sum(holder * labels[None, :], axis=1)
    target = jnp.sum(onehot * position[None, :], axis=1) * slot + rank
    buffer = jnp.zeros((rois * slot, fr_dev), jnp.float32).at[target].set(frames.T)
    buffer = buffer.reshape(npix, roi_dev, slot, fr_dev)
    local_counts = jnp.sum(onehot, axis=0)
    slot_counts = (
        jnp.sum(holder * local_counts[:, None], axis=0).astype(jnp.float32).reshape(npix, roi_dev)
    )
    own, arrived_counts = (
        lax.all_to_all(buffer, "pix", split_axis=0, concat_axis=0, tiled=True),
        lax.all_to_all(slot_counts, "pix", split_axis=0, concat_axis=0, tiled=True),
    )
    total = jnp.sum(arrived_counts, axis=0)
    own_sums = jnp.sum(own, axis=(0, 2))
    me = lax.axis_index("frame")
    width = fr_dev * nframe

    def make_tile(block):
        gram = jnp.einsum(
            "skpa,skpb->kab",
            own,
            block,
            precision=lax.Precision.HIGHEST,
            preferred_element_type=jnp.float32,
        )
        other = jnp.sum(block, axis=(0, 2))
        return total[:, None, None] * gram / (own_sums[:, :, None] * other[:, None, :])

    def place(result, block, start):
        tile = make_tile(block)
        return lax.dynamic_update_slice(result, tile, (jnp.int32(0), jnp.int32(0), start))

    result = jnp.zeros((roi_dev, fr_dev, width), jnp.float32)
    result = place(result, own, me * fr_dev)

    def turn(step, carry):
        moving, partial_out = carry
        moving = shifted(moving, "frame", 1)
        column = (me - step) % nframe
        return (moving, place(partial_out, moving, column * fr_dev))

    moving, result = lax.fori_loop(1, nframe, turn, (own, result))
    return result


def solution(mesh):
    placed = (P("frame", "pix"), P("pix", None), P())
    return jax.shard_map(
        per_device, mesh=mesh, in_specs=placed, out_specs=P("pix", "frame", None), check_vma=False
    )
```

profile of v0, /device:TPU:0, one launch (start us, length us, event | category | flops | bytes accessed | tf_op | source)
XLA Modules:
  0.0 101.8 jit_solution(17679122632339302760)
XLA Ops:
  0.0 0.7 compare_convert_fusion
  0.7 1.2 %reduce-window.6 = s32[4,2,128]{2,1,0:T(2,128)S(1)} reduce-window(s32[4,2,128]{2,1,0:T(2,128)S(1)} %compare_convert_fusion, s32[]{:T(128)} %constant.95.clone.1), window={size=1x1x128 pad=0_0x0_0x127_0}, to_apply=%region_2.3 | reduce-window | flops 130048 | bytes 8196 | tf_op jit(solution)/shard_map/reduce-window
  1.9 0.1 slice.8
  2.0 0.1 copy.17
  2.1 0.1 copy.18
  2.2 0.1 add_bitcast_fusion
  2.3 0.8 select_reduce_fusion.2
  3.1 0.9 convert_reduce_fusion
  3.9 0.7 select_reduce_fusion.1
  4.7 0.7 copy.21
  5.4 6.3 %all-to-all-start.1 = ((f32[4,1,1]{2,1,0:T(1,128)}), f32[4,1,1]{2,1,0:T(1,128)S(1)}, u32[]{:S(2)}, u32[]{:S(2)}) async-start(f32[4,1,1]{2,1,0:T(1,128)} %copy.21), calls=%async_computation.1 | async-start | bytes 4096 | tf_op jit(solution)/shard_map/all_to_all | solution.py:37
  11.7 1.1 %copy.19 = f32[256,256]{1,0:T(8,128)S(1)} copy(f32[256,256]{0,1:T(8,128)} %bitcast.82) | data formatting | bytes 524288 | tf_op jit(solution)/shard_map/transpose | solution.py:29
  12.8 2.1 %scatter_custom_fusion = f32[384,256]{1,0:T(8,128)} fusion(s32[256]{0:T(256)S(1)} %bitcast.89, f32[256,256]{1,0:T(8,128)S(1)} %copy.19, f32[]{:T(128)} %constant.96.clone.1), kind=kCustom, calls=%fused_computation.14 | custom fusion | bytes 393220 | tf_op jit(solution)/shard_map/scatter | solution.py:29
  14.9 2.2 %all-to-all-done.1 = f32[4,1,1]{2,1,0:T(1,128)S(1)} async-done(((f32[4,1,1]{2,1,0:T(1,128)}), f32[4,1,1]{2,1,0:T(1,128)S(1)}, u32[]{:S(2)}, u32[]{:S(2)}) %all-to-all-start.1) | async-done | bytes 48 | tf_op jit(solution)/shard_map/all_to_all | solution.py:37
  17.1 3.5 %all-to-all-start = ((f32[4,1,96,256]{3,2,1,0:T(8,128)}), f32[4,1,96,256]{3,2,1,0:T(8,128)S(1)}, u32[]{:S(2)}, u32[]{:S(2)}) async-start(f32[4,1,96,256]{3,2,1,0:T(8,128)} %bitcast.14), calls=%async_computation | async-start | bytes 786432 | tf_op jit(solution)/shard_map/all_to_all | solution.py:36
  20.6 0.6 reduce_sum.87
  21.2 10.0 %all-to-all-done = f32[4,1,96,256]{3,2,1,0:T(8,128)S(1)} async-done(((f32[4,1,96,256]{3,2,1,0:T(8,128)}), f32[4,1,96,256]{3,2,1,0:T(8,128)S(1)}, u32[]{:S(2)}, u32[]{:S(2)}) %all-to-all-start) | async-done | bytes 393248 | tf_op jit(solution)/shard_map/all_to_all | solution.py:36
  31.3 0.1 reduce_sum.88
  31.3 0.2 broadcast_in_dim.11
  31.6 1.4 %fusion.9 = f32[1,256,2048]{2,1,0:T(8,128)S(1)} fusion(f32[1,256,2048]{2,1,0:T(8,128)S(1)} %broadcast_in_dim.11, s32[]{:T(128)S(6)} %select_n.44, f32[4,1,96,256]{3,2,1,0:T(8,128)S(1)} %all-to-all-done, f32[256]{0:T(256)S(1)} %reduce_sum.88, f32[]{:T(128)} %reduce_sum.87), kind=kOutput, calls=%fused_computation.12 | convolution fusion | flops 302186496 | bytes 657416 | tf_op jit(solution)/shard_map/skpa,skpb->kab/dot_general | solution.py:45
  33.0 67.5 %while.17 = (s32[]{:T(128)}, f32[4,1,96,256]{3,2,0,1:T(8,128)S(1)}, f32[1,256,2048]{2,1,0:T(8,128)S(1)}, f32[1]{0:T(128)}, f32[4,1,96,256]{3,2,0,1:T(8,128)S(1)}...) while((s32[]{:T(128)}, f32[4,1,96,256]{3,2,0,1:T(8,128)S(1)}, ...), condition=%wide.region_12.13_spmd, body=%wide.region_10.12_spmd.sunk | while | flops 302284576 | bytes 3804512 | solution.py:68
  33.0 0.1 collective-permute-start
  33.1 8.1 %collective-permute-done = f32[4,1,96,256]{3,2,0,1:T(8,128)S(1)} collective-permute-done((f32[4,1,96,256]{3,2,0,1:T(8,128)S(1)}, f32[4,1,96,256]{3,2,0,1:T(8,128)S(1)}, u32[]{:S(2)}, u32[]{:S(2)}) %collective-permute-start) | collective-permute-done | bytes 393248 | tf_op jit(solution)/shard_map/while/body/eval_jaxpr/ppermute | solution.py:12
  41.2 0.1 reduce_sum.97
  41.2 1.4 %fusion.20 = f32[1,256,2048]{2,1,0:T(8,128)S(1)} fusion(f32[1,256,2048]{2,1,0:T(8,128)S(1)} %get-tuple-element.273, s32[]{:T(128)S(6)} %select_n.49, f32[4,1,96,256]{3,2,0,1:T(8,128)S(1)} %collective-permute-done, f32[4,1,96,256]{3,2,0,1:T(8,128)S(1)} %get-tuple-element.289, f32[256]{0:T(256)S(1)} %reduce_sum.97, f32[256]{0:T(256)S(1)} %bitcast.88, ...), kind=kOutput, calls=%fused_computation.5.clone.1 | convolution fusion | flops 302186496 | bytes 1050632 | tf_op jit(solution)/shard_map/while/body/eval_jaxpr/skpa,skpb->kab/dot_general | solution.py:45
  42.6 0.1 collective-permute-start
  42.7 8.1 %collective-permute-done = f32[4,1,96,256]{3,2,0,1:T(8,128)S(1)} collective-permute-done((f32[4,1,96,256]{3,2,0,1:T(8,128)S(1)}, f32[4,1,96,256]{3,2,0,1:T(8,128)S(1)}, u32[]{:S(2)}, u32[]{:S(2)}) %collective-permute-start) | collective-permute-done | bytes 393248 | tf_op jit(solution)/shard_map/while/body/eval_jaxpr/ppermute | solution.py:12
  50.8 0.1 reduce_sum.97
  50.9 1.4 %fusion.20 = f32[1,256,2048]{2,1,0:T(8,128)S(1)} fusion(f32[1,256,2048]{2,1,0:T(8,128)S(1)} %get-tuple-element.273, s32[]{:T(128)S(6)} %select_n.49, f32[4,1,96,256]{3,2,0,1:T(8,128)S(1)} %collective-permute-done, f32[4,1,96,256]{3,2,0,1:T(8,128)S(1)} %get-tuple-element.289, f32[256]{0:T(256)S(1)} %reduce_sum.97, f32[256]{0:T(256)S(1)} %bitcast.88, ...), kind=kOutput, calls=%fused_computation.5.clone.1 | convolution fusion | flops 302186496 | bytes 1050632 | tf_op jit(solution)/shard_map/while/body/eval_jaxpr/skpa,skpb->kab/dot_general | solution.py:45
  52.3 0.1 collective-permute-start
  52.3 8.1 %collective-permute-done = f32[4,1,96,256]{3,2,0,1:T(8,128)S(1)} collective-permute-done((f32[4,1,96,256]{3,2,0,1:T(8,128)S(1)}, f32[4,1,96,256]{3,2,0,1:T(8,128)S(1)}, u32[]{:S(2)}, u32[]{:S(2)}) %collective-permute-start) | collective-permute-done | bytes 393248 | tf_op jit(solution)/shard_map/while/body/eval_jaxpr/ppermute | solution.py:12
  60.4 0.1 reduce_sum.97
  60.5 1.4 %fusion.20 = f32[1,256,2048]{2,1,0:T(8,128)S(1)} fusion(f32[1,256,2048]{2,1,0:T(8,128)S(1)} %get-tuple-element.273, s32[]{:T(128)S(6)} %select_n.49, f32[4,1,96,256]{3,2,0,1:T(8,128)S(1)} %collective-permute-done, f32[4,1,96,256]{3,2,0,1:T(8,128)S(1)} %get-tuple-element.289, f32[256]{0:T(256)S(1)} %reduce_sum.97, f32[256]{0:T(256)S(1)} %bitcast.88, ...), kind=kOutput, calls=%fused_computation.5.clone.1 | convolution fusion | flops 302186496 | bytes 1050632 | tf_op jit(solution)/shard_map/while/body/eval_jaxpr/skpa,skpb->kab/dot_general | solution.py:45
  61.9 0.1 collective-permute-start
  62.0 8.1 %collective-permute-done = f32[4,1,96,256]{3,2,0,1:T(8,128)S(1)} collective-permute-done((f32[4,1,96,256]{3,2,0,1:T(8,128)S(1)}, f32[4,1,96,256]{3,2,0,1:T(8,128)S(1)}, u32[]{:S(2)}, u32[]{:S(2)}) %collective-permute-start) | collective-permute-done | bytes 393248 | tf_op jit(solution)/shard_map/while/body/eval_jaxpr/ppermute | solution.py:12
  70.1 0.1 reduce_sum.97
  70.1 1.4 %fusion.20 = f32[1,256,2048]{2,1,0:T(8,128)S(1)} fusion(f32[1,256,2048]{2,1,0:T(8,128)S(1)} %get-tuple-element.273, s32[]{:T(128)S(6)} %select_n.49, f32[4,1,96,256]{3,2,0,1:T(8,128)S(1)} %collective-permute-done, f32[4,1,96,256]{3,2,0,1:T(8,128)S(1)} %get-tuple-element.289, f32[256]{0:T(256)S(1)} %reduce_sum.97, f32[256]{0:T(256)S(1)} %bitcast.88, ...), kind=kOutput, calls=%fused_computation.5.clone.1 | convolution fusion | flops 302186496 | bytes 1050632 | tf_op jit(solution)/shard_map/while/body/eval_jaxpr/skpa,skpb->kab/dot_general | solution.py:45
  71.5 0.1 collective-permute-start
  71.6 8.1 %collective-permute-done = f32[4,1,96,256]{3,2,0,1:T(8,128)S(1)} collective-permute-done((f32[4,1,96,256]{3,2,0,1:T(8,128)S(1)}, f32[4,1,96,256]{3,2,0,1:T(8,128)S(1)}, u32[]{:S(2)}, u32[]{:S(2)}) %collective-permute-start) | collective-permute-done | bytes 393248 | tf_op jit(solution)/shard_map/while/body/eval_jaxpr/ppermute | solution.py:12
  79.7 0.1 reduce_sum.97
  79.8 1.4 %fusion.20 = f32[1,256,2048]{2,1,0:T(8,128)S(1)} fusion(f32[1,256,2048]{2,1,0:T(8,128)S(1)} %get-tuple-element.273, s32[]{:T(128)S(6)} %select_n.49, f32[4,1,96,256]{3,2,0,1:T(8,128)S(1)} %collective-permute-done, f32[4,1,96,256]{3,2,0,1:T(8,128)S(1)} %get-tuple-element.289, f32[256]{0:T(256)S(1)} %reduce_sum.97, f32[256]{0:T(256)S(1)} %bitcast.88, ...), kind=kOutput, calls=%fused_computation.5.clone.1 | convolution fusion | flops 302186496 | bytes 1050632 | tf_op jit(solution)/shard_map/while/body/eval_jaxpr/skpa,skpb->kab/dot_general | solution.py:45
  81.2 0.1 collective-permute-start
  81.3 8.1 %collective-permute-done = f32[4,1,96,256]{3,2,0,1:T(8,128)S(1)} collective-permute-done((f32[4,1,96,256]{3,2,0,1:T(8,128)S(1)}, f32[4,1,96,256]{3,2,0,1:T(8,128)S(1)}, u32[]{:S(2)}, u32[]{:S(2)}) %collective-permute-start) | collective-permute-done | bytes 393248 | tf_op jit(solution)/shard_map/while/body/eval_jaxpr/ppermute | solution.py:12
  89.4 0.1 reduce_sum.97
  89.4 1.4 %fusion.20 = f32[1,256,2048]{2,1,0:T(8,128)S(1)} fusion(f32[1,256,2048]{2,1,0:T(8,128)S(1)} %get-tuple-element.273, s32[]{:T(128)S(6)} %select_n.49, f32[4,1,96,256]{3,2,0,1:T(8,128)S(1)} %collective-permute-done, f32[4,1,96,256]{3,2,0,1:T(8,128)S(1)} %get-tuple-element.289, f32[256]{0:T(256)S(1)} %reduce_sum.97, f32[256]{0:T(256)S(1)} %bitcast.88, ...), kind=kOutput, calls=%fused_computation.5.clone.1 | convolution fusion | flops 302186496 | bytes 1050632 | tf_op jit(solution)/shard_map/while/body/eval_jaxpr/skpa,skpb->kab/dot_general | solution.py:45
  90.8 0.1 collective-permute-start
  90.9 8.1 %collective-permute-done = f32[4,1,96,256]{3,2,0,1:T(8,128)S(1)} collective-permute-done((f32[4,1,96,256]{3,2,0,1:T(8,128)S(1)}, f32[4,1,96,256]{3,2,0,1:T(8,128)S(1)}, u32[]{:S(2)}, u32[]{:S(2)}) %collective-permute-start) | collective-permute-done | bytes 393248 | tf_op jit(solution)/shard_map/while/body/eval_jaxpr/ppermute | solution.py:12
  99.0 0.1 reduce_sum.97
  99.1 1.4 %fusion.20 = f32[1,256,2048]{2,1,0:T(8,128)S(1)} fusion(f32[1,256,2048]{2,1,0:T(8,128)S(1)} %get-tuple-element.273, s32[]{:T(128)S(6)} %select_n.49, f32[4,1,96,256]{3,2,0,1:T(8,128)S(1)} %collective-permute-done, f32[4,1,96,256]{3,2,0,1:T(8,128)S(1)} %get-tuple-element.289, f32[256]{0:T(256)S(1)} %reduce_sum.97, f32[256]{0:T(256)S(1)} %bitcast.88, ...), kind=kOutput, calls=%fused_computation.5.clone.1 | convolution fusion | flops 302186496 | bytes 1050632 | tf_op jit(solution)/shard_map/while/body/eval_jaxpr/skpa,skpb->kab/dot_general | solution.py:45
  100.5 0.0 copy-start
  100.5 1.3 %copy-done = f32[1,256,2048]{2,1,0:T(8,128)} copy-done((f32[1,256,2048]{2,1,0:T(8,128)}, f32[1,256,2048]{2,1,0:T(8,128)S(1)}, u32[]{:S(2)}) %copy-start) | copy-done | bytes 2097176
  (13 shorter events, 0.3 us)
Async XLA Ops:
  5.4 11.8 %all-to-all-start.1 = ((f32[4,1,1]{2,1,0:T(1,128)}), f32[4,1,1]{2,1,0:T(1,128)S(1)}, u32[]{:S(2)}, u32[]{:S(2)}) async-start(f32[4,1,1]{2,1,0:T(1,128)} %copy.21), calls=%async_computation.1 | async-start | bytes 4096 | tf_op jit(solution)/shard_map/all_to_all | solution.py:37
  17.1 14.1 %all-to-all-start = ((f32[4,1,96,256]{3,2,1,0:T(8,128)}), f32[4,1,96,256]{3,2,1,0:T(8,128)S(1)}, u32[]{:S(2)}, u32[]{:S(2)}) async-start(f32[4,1,96,256]{3,2,1,0:T(8,128)} %bitcast.14), calls=%async_computation | async-start | bytes 786432 | tf_op jit(solution)/shard_map/all_to_all | solution.py:36
  33.0 8.2 %collective-permute-start = (f32[4,1,96,256]{3,2,0,1:T(8,128)S(1)}, f32[4,1,96,256]{3,2,0,1:T(8,128)S(1)}, u32[]{:S(2)}, u32[]{:S(2)}) collective-permute-start(f32[4,1,96,256]{3,2,0,1:T(8,128)S(1)} %get-tuple-element.272), channel_id=1, source_target_pairs={{0,4},{4,8},{8,12},{12,16},{16,20},{20,24},{24,28},{28,0},{1,5},{5... | collective-permute-start | bytes 1179656 | tf_op jit(solution)/shard_map/while/body/eval_jaxpr/ppermute | solution.py:12
  42.6 8.2 %collective-permute-start = (f32[4,1,96,256]{3,2,0,1:T(8,128)S(1)}, f32[4,1,96,256]{3,2,0,1:T(8,128)S(1)}, u32[]{:S(2)}, u32[]{:S(2)}) collective-permute-start(f32[4,1,96,256]{3,2,0,1:T(8,128)S(1)} %get-tuple-element.272), channel_id=1, source_target_pairs={{0,4},{4,8},{8,12},{12,16},{16,20},{20,24},{24,28},{28,0},{1,5},{5... | collective-permute-start | bytes 1179656 | tf_op jit(solution)/shard_map/while/body/eval_jaxpr/ppermute | solution.py:12
  52.3 8.2 %collective-permute-start = (f32[4,1,96,256]{3,2,0,1:T(8,128)S(1)}, f32[4,1,96,256]{3,2,0,1:T(8,128)S(1)}, u32[]{:S(2)}, u32[]{:S(2)}) collective-permute-start(f32[4,1,96,256]{3,2,0,1:T(8,128)S(1)} %get-tuple-element.272), channel_id=1, source_target_pairs={{0,4},{4,8},{8,12},{12,16},{16,20},{20,24},{24,28},{28,0},{1,5},{5... | collective-permute-start | bytes 1179656 | tf_op jit(solution)/shard_map/while/body/eval_jaxpr/ppermute | solution.py:12
  61.9 8.2 %collective-permute-start = (f32[4,1,96,256]{3,2,0,1:T(8,128)S(1)}, f32[4,1,96,256]{3,2,0,1:T(8,128)S(1)}, u32[]{:S(2)}, u32[]{:S(2)}) collective-permute-start(f32[4,1,96,256]{3,2,0,1:T(8,128)S(1)} %get-tuple-element.272), channel_id=1, source_target_pairs={{0,4},{4,8},{8,12},{12,16},{16,20},{20,24},{24,28},{28,0},{1,5},{5... | collective-permute-start | bytes 1179656 | tf_op jit(solution)/shard_map/while/body/eval_jaxpr/ppermute | solution.py:12
  71.5 8.2 %collective-permute-start = (f32[4,1,96,256]{3,2,0,1:T(8,128)S(1)}, f32[4,1,96,256]{3,2,0,1:T(8,128)S(1)}, u32[]{:S(2)}, u32[]{:S(2)}) collective-permute-start(f32[4,1,96,256]{3,2,0,1:T(8,128)S(1)} %get-tuple-element.272), channel_id=1, source_target_pairs={{0,4},{4,8},{8,12},{12,16},{16,20},{20,24},{24,28},{28,0},{1,5},{5... | collective-permute-start | bytes 1179656 | tf_op jit(solution)/shard_map/while/body/eval_jaxpr/ppermute | solution.py:12
  81.2 8.2 %collective-permute-start = (f32[4,1,96,256]{3,2,0,1:T(8,128)S(1)}, f32[4,1,96,256]{3,2,0,1:T(8,128)S(1)}, u32[]{:S(2)}, u32[]{:S(2)}) collective-permute-start(f32[4,1,96,256]{3,2,0,1:T(8,128)S(1)} %get-tuple-element.272), channel_id=1, source_target_pairs={{0,4},{4,8},{8,12},{12,16},{16,20},{20,24},{24,28},{28,0},{1,5},{5... | collective-permute-start | bytes 1179656 | tf_op jit(solution)/shard_map/while/body/eval_jaxpr/ppermute | solution.py:12
  90.8 8.2 %collective-permute-start = (f32[4,1,96,256]{3,2,0,1:T(8,128)S(1)}, f32[4,1,96,256]{3,2,0,1:T(8,128)S(1)}, u32[]{:S(2)}, u32[]{:S(2)}) collective-permute-start(f32[4,1,96,256]{3,2,0,1:T(8,128)S(1)} %get-tuple-element.272), channel_id=1, source_target_pairs={{0,4},{4,8},{8,12},{12,16},{16,20},{20,24},{24,28},{28,0},{1,5},{5... | collective-permute-start | bytes 1179656 | tf_op jit(solution)/shard_map/while/body/eval_jaxpr/ppermute | solution.py:12
  100.5 1.3 %copy-start = (f32[1,256,2048]{2,1,0:T(8,128)}, f32[1,256,2048]{2,1,0:T(8,128)S(1)}, u32[]{:S(2)}) copy-start(f32[1,256,2048]{2,1,0:T(8,128)S(1)} %get-tuple-element.301) | copy-start | bytes 6291460
where the time goes:
time: 102 us
  waiting for transfers between devices  68.7 us (67%)
  matrix products  11 us (11%)
  starting transfers between devices  10.2 us (10%)
  local copies, waits for them, and re-layouts  5.93 us (6%)
  other arithmetic  5.53 us (5%)
    ppermute x7, waiting for transfers between devices, shifted(): return lax.ppermute(value, axis, pairs)  56.4 us
    dot_general x8, matrix products, make_tile(): jnp.einsum('skpa,skpb->kab', own, block, precision=lax.Precision.HIGHEST,...  11 us
    all_to_all x1, waiting for transfers between devices, per_device(): lax.all_to_all(buffer, 'pix', split_axis=0, concat_axis=0, tiled=True)  10 us
    all_to_all x1, starting transfers between devices, per_device(): lax.all_to_all(slot_counts, 'pix', split_axis=0, concat_axis=0, tiled=True)  6.35 us
    all_to_all x1, starting transfers between devices, per_device(): lax.all_to_all(buffer, 'pix', split_axis=0, concat_axis=0, tiled=True)  3.46 us
    all_to_all x1, waiting for transfers between devices, per_device(): lax.all_to_all(slot_counts, 'pix', split_axis=0, concat_axis=0, tiled=True)  2.18 us
    scatter x1, local copies, waits for them, and re-layouts, per_device(): jnp.zeros((rois * slot, fr_dev), jnp.float32).at[target].set(frames.T)  2.14 us
  transfers between devices with their start and end apart: 9, of which 9 were waited for; matrix products, arithmetic and copies ran while one was open for 4% of the time, Pallas kernels for 0%

commit v1 on v0

--- a/solution.py
+++ b/solution.py
@@ -1,9 +1,194 @@
+import functools
+
 import jax
 import jax.numpy as jnp
 from jax import lax
+from jax.experimental import pallas as pl
+from jax.experimental.pallas import tpu as pltpu
 from jax.sharding import PartitionSpec as P
 
 SLOT = 96
+MESH = pl.DeviceIdType.MESH
+F32 = jnp.float32
+BF16 = jnp.bfloat16
+
+
+def flip(value, mask):
+    bit = 1
+    out = value
+    while bit <= mask:
+        if mask & bit:
+            out = out + bit - 2 * bit * ((value // bit) % 2)
+        bit *= 2
+    return out
+
+
+def halves(value):
+    high = value.astype(BF16)
+    return high, (value - high.astype(F32)).astype(BF16)
+
+
+def kernel(npix, order_ref, ids_ref, frames_ref, out_ref, packed, grid, lhs, cols, sems_send, sems_recv):
+    frame = lax.axis_index("frame")
+    pix = lax.axis_index("pix")
+    fr, npx = frames_ref.shape
+    slot = SLOT
+    half = slot // 2
+
+    def at_frame(mask):
+        return (flip(frame, mask), pix)
+
+    def at_pix(mask):
+        return (frame, flip(pix, mask))
+
+    peers = [at_frame(1), at_frame(2), at_frame(4)] + [at_pix(k) for k in range(1, npix)]
+    barrier = pltpu.get_barrier_semaphore()
+    for peer in peers:
+        pl.semaphore_signal(barrier, inc=1, device_id=peer, device_id_type=MESH)
+
+    below = lax.broadcasted_iota(jnp.int32, (npx, npx), 0)
+    across = lax.broadcasted_iota(jnp.int32, (npx, npx), 1)
+    column = jnp.broadcast_to(ids_ref[...], (npx, npx))
+    row = jnp.sum(jnp.where(below == across, column, 0), axis=0, keepdims=True)
+    earlier = jnp.logical_and(column == row, below < across)
+    rank = jnp.sum(earlier.astype(jnp.int32), axis=0, keepdims=True)
+    place = lax.broadcasted_iota(jnp.int32, (slot, npx), 0)
+    picks = []
+    for k in range(npix):
+        region = order_ref[flip(pix, k)]
+        wanted = jnp.where(row == region, rank, -1)
+        picks.append((wanted == place).astype(F32).astype(BF16))
+    pick = jnp.concatenate(picks, axis=0)
+    rest = frames_ref[...]
+    total = None
+    for _ in range(3):
+        piece = rest.astype(BF16)
+        rest = rest - piece.astype(F32)
+        part = lax.dot_general(pick, piece, (((1,), (1,)), ((), ())), preferred_element_type=F32)
+        total = part if total is None else total + part
+    for k in range(1, npix):
+        packed[k - 1] = total[k * slot:(k + 1) * slot]
+    grid[0, 0] = total[:slot]
+
+    pl.semaphore_wait(barrier, len(peers))
+
+    copies = []
+
+    def send(source, target, peer):
+        number = len(copies)
+        copy = pltpu.make_async_remote_copy(
+            src_ref=source,
+            dst_ref=target,
+            send_sem=sems_send.at[number],
+            recv_sem=sems_recv.at[number],
+            device_id=peer,
+            device_id_type=MESH,
+        )
+        copy.start()
+        copies.append(copy)
+        return copy
+
+    low, high = pl.ds(0, half), pl.ds(half, half)
+    arrive = {}
+
+    def spread(k):
+        arrive["x", k] = send(grid.at[0, k], grid.at[2, k], at_frame(2))
+        arrive["y", k] = send(grid.at[0, k], grid.at[4, k], at_frame(4))
+        arrive[1, k] = send(grid.at[0, k], grid.at[1, k], at_frame(1))
+
+    def relay(k):
+        arrive["x", k].wait_recv()
+        arrive["low", k] = send(grid.at[2, k, low], grid.at[6, k, low], at_frame(4))
+        arrive[3, k] = send(grid.at[2, k], grid.at[3, k], at_frame(1))
+        arrive["y", k].wait_recv()
+        arrive["high", k] = send(grid.at[4, k, high], grid.at[6, k, high], at_frame(2))
+        arrive[5, k] = send(grid.at[4, k], grid.at[5, k], at_frame(1))
+
+    def corner(k):
+        arrive["low", k].wait_recv()
+        arrive["high", k].wait_recv()
+        arrive[7, k] = send(grid.at[6, k], grid.at[7, k], at_frame(1))
+
+    state = {"sum": None, "count": None}
+
+    def own(k):
+        value = jnp.transpose(grid[0, k])
+        sums = jnp.sum(value, axis=1, keepdims=True)
+        count = jnp.sum((value > 0).astype(F32), axis=1, keepdims=True)
+        state["sum"] = sums if k == 0 else state["sum"] + sums
+        state["count"] = count if k == 0 else state["count"] + count
+        top, bottom = halves(value)
+        lhs[k] = jnp.concatenate([top, bottom, top], axis=1)
+
+    def tile(r, k):
+        value = grid[r, k]
+        sums = jnp.sum(value, axis=0, keepdims=True)
+        top, bottom = halves(value)
+        rhs = jnp.concatenate([top, top, bottom], axis=0)
+        part = jnp.dot(lhs[k], rhs, preferred_element_type=F32)
+        where = pl.ds(pl.multiple_of(flip(frame, r) * fr, fr), fr)
+        if k > 0:
+            part = out_ref[0, :, where] + part
+            sums = cols[r] + sums
+        if k == npix - 1:
+            part = part * state["row"] * (1.0 / sums)
+        else:
+            cols[r] = sums
+        out_ref[0, :, where] = part
+
+    def tiles(k, near):
+        if near:
+            own(k)
+            if k == npix - 1:
+                state["row"] = state["count"] / state["sum"]
+            arrive[1, k].wait_recv()
+            rels = (0, 1, 2, 4)
+        else:
+            for r in (3, 5, 7):
+                arrive[r, k].wait_recv()
+            rels = (6, 3, 5, 7)
+        for r in rels:
+            tile(r, k)
+
+    incoming = {k: send(packed.at[k - 1], grid.at[0, k], at_pix(k)) for k in range(1, npix)}
+    spread(0)
+    for k in range(npix):
+        if k + 1 < npix:
+            incoming[k + 1].wait_recv()
+            spread(k + 1)
+        relay(k)
+        if k > 0:
+            corner(k - 1)
+            tiles(k - 1, False)
+        tiles(k, True)
+    corner(npix - 1)
+    tiles(npix - 1, False)
+    for copy in copies:
+        copy.wait_send()
+
+
+def fused(npix, frames, roi_ids, roi_order):
+    fr, npx = frames.shape
+    slot = SLOT
+    count = (npix - 1) + 9 * npix
+    vmem = pl.BlockSpec(memory_space=pltpu.VMEM)
+    return pl.pallas_call(
+        functools.partial(kernel, npix),
+        out_shape=jax.ShapeDtypeStruct((1, fr, 8 * fr), F32),
+        in_specs=[pl.BlockSpec(memory_space=pltpu.SMEM), vmem, vmem],
+        out_specs=vmem,
+        scratch_shapes=[
+            pltpu.VMEM((npix - 1, slot, fr), F32),
+            pltpu.VMEM((8, npix, slot, fr), F32),
+            pltpu.VMEM((npix, fr, 3 * slot), BF16),
+            pltpu.VMEM((8, 1, fr), F32),
+            pltpu.SemaphoreType.DMA((count,)),
+            pltpu.SemaphoreType.DMA((count,)),
+        ],
+        compiler_params=pltpu.CompilerParams(
+            collective_id=0, has_side_effects=True, vmem_limit_bytes=40 * 1024 * 1024
+        ),
+    )(roi_order, roi_ids, frames)
 
 
 def shifted(value, axis, steps):
@@ -70,7 +255,15 @@
 
 
 def solution(mesh):
+    npix, nframe = mesh.shape["pix"], mesh.shape["frame"]
     placed = (P("frame", "pix"), P("pix", None), P())
+
+    def body(frames, roi_ids, roi_order):
+        paired = nframe == 8 and npix & (npix - 1) == 0 and roi_order.shape[0] == npix
+        if paired:
+            return fused(npix, frames, roi_ids, roi_order)
+        return per_device(frames, roi_ids, roi_order)
+
     return jax.shard_map(
-        per_device, mesh=mesh, in_specs=placed, out_specs=P("pix", "frame", None), check_vma=False
+        body, mesh=mesh, in_specs=placed, out_specs=P("pix", "frame", None), check_vma=False
     )

time: 102 us -> 31.6 us (0.31)
  waiting for transfers between devices: 68.7 us -> 0 us
  Pallas kernels: 0 us -> 27.6 us
  matrix products: 11 us -> 0 us
  starting transfers between devices: 10.2 us -> 0 us
  other arithmetic: 5.53 us -> 0 us
  local copies, waits for them, and re-layouts: 5.93 us -> 3.73 us
    ppermute x7 -> x0, waiting for transfers between devices: 56.4 us -> none  [shifted(): return lax.ppermute(value, axis, pairs)]
    pallas_call x0 -> x1, Pallas kernels: none -> 27.6 us  [fused(): pl.pallas_call(functools.partial(kernel, npix), out_shape=jax.ShapeDtypeS...]
    all_to_all x2 -> x0, waiting for transfers between devices: 12.2 us -> none  [the longest x1 10 us: per_device(): lax.all_to_all(buffer, 'pix', split_axis=0, concat_axis=0, tiled=True)]
    dot_general x8 -> x0, matrix products: 11 us -> none  [make_tile(): jnp.einsum('skpa,skpb->kab', own, block, precision=lax.Precision.HIGHEST,...]
    all_to_all x2 -> x0, starting transfers between devices: 9.81 us -> none  [the longest x1 6.35 us: per_device(): lax.all_to_all(slot_counts, 'pix', split_axis=0, concat_axis=0, tiled=True)]
    reduce_sum x12 -> x0, other arithmetic: 3.51 us -> none  [the longest x1 0.87 us: per_device(): local_counts = jnp.sum(onehot, axis=0)]
    unnamed x3 -> x6, local copies, waits for them, and re-layouts: 1.34 us -> 3.73 us
    scatter x1 -> x0, local copies, waits for them, and re-layouts: 2.14 us -> none  [per_device(): jnp.zeros((rois * slot, fr_dev), jnp.float32).at[target].set(frames.T)]
  transfers between devices with their start and end apart: 9 -> 0, of which waited for: 9 -> 0; matrix products, arithmetic and copies ran while one was open for 4% -> 0% of each run, Pallas kernels for 0% -> 0%
where the time goes in v1:
time: 31.6 us; the launch traced here: 31.4 us
  Pallas kernels  27.6 us (87%)
  local copies, waits for them, and re-layouts  3.73 us (12%)
    pallas_call x1, Pallas kernels, fused(): pl.pallas_call(functools.partial(kernel, npix), out_shape=jax.ShapeDtypeS...  27.6 us
    unnamed x6, local copies, waits for them, and re-layouts  3.73 us

profile of v1, /device:TPU:0, one launch (start us, length us, event | category | flops | bytes accessed | tf_op | source)
XLA Modules:
  0.0 31.4 jit_solution(11016878362169051488)
XLA Ops:
  0.0 0.8 %copy.4.ids_ref = s32[256,1]{1,0:T(8,128)S(1)} copy(s32[256,1]{0,1:T(1,128)} %param.4) | data formatting | bytes 2048 | tf_op args[1]
  0.8 0.0 copy-start
  0.8 0.9 %copy-done = f32[256,256]{1,0:T(8,128)S(1)} copy-done((f32[256,256]{1,0:T(8,128)S(1)}, f32[256,256]{1,0:T(8,128)}, u32[]{:S(2)}) %copy-start) | copy-done | bytes 262168
  1.8 0.0 copy-start.1
  1.8 0.7 %copy-done.1 = s32[4]{0:T(128)S(1)} copy-done((s32[4]{0:T(128)S(1)}, s32[4]{0:T(128)}, u32[]{:S(2)}) %copy-start.1) | copy-done | bytes 40
  2.4 27.6 %shard_map.37 = f32[1,256,2048]{2,1,0:T(8,128)S(1)} custom-call(s32[4]{0:T(128)S(1)} %copy-done.1, s32[256,1]{1,0:T(8,128)S(1)} %copy.4.ids_ref, f32[256,256]{1,0:T(8,128)S(1)} %copy-done), custom_call_target="tpu_custom_call" | custom-call | tf_op jit(solution)/shard_map/pallas_call | solution.py:175
  30.1 1.3 %copy.6 = f32[1,256,2048]{2,1,0:T(8,128)} copy(f32[1,256,2048]{2,1,0:T(8,128)S(1)} %shard_map.37) | data formatting | bytes 4194304
Async XLA Ops:
  0.8 1.0 %copy-start = (f32[256,256]{1,0:T(8,128)S(1)}, f32[256,256]{1,0:T(8,128)}, u32[]{:S(2)}) copy-start(f32[256,256]{1,0:T(8,128)} %frames_ref.1) | copy-start | bytes 786436
  1.8 0.7 %copy-start.1 = (s32[4]{0:T(128)S(1)}, s32[4]{0:T(128)}, u32[]{:S(2)}) copy-start(s32[4]{0:T(128)} %order_ref.1) | copy-start | bytes 52

commit v2 on v1

--- a/solution.py
+++ b/solution.py
@@ -8,6 +8,10 @@
 from jax.sharding import PartitionSpec as P
 
 SLOT = 96
+PIECES = 2
+LEAD = 2
+LAG = 2
+WHOLE = 0
 MESH = pl.DeviceIdType.MESH
 F32 = jnp.float32
 BF16 = jnp.bfloat16
@@ -28,12 +32,24 @@
     return high, (value - high.astype(F32)).astype(BF16)
 
 
-def kernel(npix, order_ref, ids_ref, frames_ref, out_ref, packed, grid, lhs, cols, sems_send, sems_recv):
+def kernel(
+    npix, order_hbm, ids_hbm, frames_hbm, out_ref, order_ref, ids_ref, frames_ref, packed, grid, lhs, cols,
+    sems_load, sems_send, sems_recv
+):
     frame = lax.axis_index("frame")
     pix = lax.axis_index("pix")
     fr, npx = frames_ref.shape
+    loads = [
+        pltpu.make_async_copy(source, target, sems_load.at[number])
+        for number, (source, target) in enumerate(
+            ((ids_hbm, ids_ref), (order_hbm, order_ref), (frames_hbm, frames_ref))
+        )
+    ]
+    for load in loads:
+        load.start()
     slot = SLOT
-    half = slot // 2
+    step = slot // PIECES
+    half = step // 2
 
     def at_frame(mask):
         return (flip(frame, mask), pix)
@@ -48,17 +64,20 @@
 
     below = lax.broadcasted_iota(jnp.int32, (npx, npx), 0)
     across = lax.broadcasted_iota(jnp.int32, (npx, npx), 1)
-    column = jnp.broadcast_to(ids_ref[...], (npx, npx))
-    row = jnp.sum(jnp.where(below == across, column, 0), axis=0, keepdims=True)
+    loads[0].wait()
+    row = ids_ref[...]
+    column = jnp.sum(jnp.where(below == across, row, 0), axis=1, keepdims=True)
     earlier = jnp.logical_and(column == row, below < across)
     rank = jnp.sum(earlier.astype(jnp.int32), axis=0, keepdims=True)
     place = lax.broadcasted_iota(jnp.int32, (slot, npx), 0)
     picks = []
+    loads[1].wait()
     for k in range(npix):
         region = order_ref[flip(pix, k)]
         wanted = jnp.where(row == region, rank, -1)
         picks.append((wanted == place).astype(F32).astype(BF16))
     pick = jnp.concatenate(picks, axis=0)
+    loads[2].wait()
     rest = frames_ref[...]
     total = None
     for _ in range(3):
@@ -88,26 +107,42 @@
         copies.append(copy)
         return copy
 
-    low, high = pl.ds(0, half), pl.ds(half, half)
     arrive = {}
 
-    def spread(k):
-        arrive["x", k] = send(grid.at[0, k], grid.at[2, k], at_frame(2))
-        arrive["y", k] = send(grid.at[0, k], grid.at[4, k], at_frame(4))
-        arrive[1, k] = send(grid.at[0, k], grid.at[1, k], at_frame(1))
-
-    def relay(k):
-        arrive["x", k].wait_recv()
-        arrive["low", k] = send(grid.at[2, k, low], grid.at[6, k, low], at_frame(4))
-        arrive[3, k] = send(grid.at[2, k], grid.at[3, k], at_frame(1))
-        arrive["y", k].wait_recv()
-        arrive["high", k] = send(grid.at[4, k, high], grid.at[6, k, high], at_frame(2))
-        arrive[5, k] = send(grid.at[4, k], grid.at[5, k], at_frame(1))
-
-    def corner(k):
-        arrive["low", k].wait_recv()
-        arrive["high", k].wait_recv()
-        arrive[7, k] = send(grid.at[6, k], grid.at[7, k], at_frame(1))
+    def rows(piece):
+        return pl.ds(piece * step, step)
+
+    def spread(k, piece):
+        part = rows(piece)
+        arrive["x", k, piece] = send(grid.at[0, k, part], grid.at[2, k, part], at_frame(2))
+        arrive["y", k, piece] = send(grid.at[0, k, part], grid.at[4, k, part], at_frame(4))
+        arrive[1, k, piece] = send(grid.at[0, k, part], grid.at[1, k, part], at_frame(1))
+
+    def relay(k, piece):
+        part = rows(piece)
+        number = k * PIECES + piece
+        low, high = pl.ds(piece * step, half), pl.ds(piece * step + half, half)
+        if number < WHOLE:
+            low, high = (part, None) if number % 2 == 0 else (None, part)
+        arrive["x", k, piece].wait_recv()
+        if low is not None:
+            arrive["low", k, piece] = send(grid.at[2, k, low], grid.at[6, k, low], at_frame(4))
+        arrive[3, k, piece] = send(grid.at[2, k, part], grid.at[3, k, part], at_frame(1))
+        arrive["y", k, piece].wait_recv()
+        if high is not None:
+            arrive["high", k, piece] = send(grid.at[4, k, high], grid.at[6, k, high], at_frame(2))
+        arrive[5, k, piece] = send(grid.at[4, k, part], grid.at[5, k, part], at_frame(1))
+
+    def corner(k, piece):
+        for way in ("low", "high"):
+            if (way, k, piece) in arrive:
+                arrive[way, k, piece].wait_recv()
+        part = rows(piece)
+        arrive[7, k, piece] = send(grid.at[6, k, part], grid.at[7, k, part], at_frame(1))
+
+    def landed(r, k):
+        for piece in range(PIECES):
+            arrive[r, k, piece].wait_recv()
 
     state = {"sum": None, "count": None}
 
@@ -136,33 +171,57 @@
             cols[r] = sums
         out_ref[0, :, where] = part
 
-    def tiles(k, near):
-        if near:
-            own(k)
-            if k == npix - 1:
-                state["row"] = state["count"] / state["sum"]
-            arrive[1, k].wait_recv()
-            rels = (0, 1, 2, 4)
-        else:
-            for r in (3, 5, 7):
-                arrive[r, k].wait_recv()
-            rels = (6, 3, 5, 7)
-        for r in rels:
+    def near(k):
+        own(k)
+        if k == npix - 1:
+            state["row"] = state["count"] / state["sum"]
+        for r in (0, 2, 4):
             tile(r, k)
-
-    incoming = {k: send(packed.at[k - 1], grid.at[0, k], at_pix(k)) for k in range(1, npix)}
-    spread(0)
-    for k in range(npix):
-        if k + 1 < npix:
-            incoming[k + 1].wait_recv()
-            spread(k + 1)
-        relay(k)
-        if k > 0:
-            corner(k - 1)
-            tiles(k - 1, False)
-        tiles(k, True)
-    corner(npix - 1)
-    tiles(npix - 1, False)
+        landed(1, k)
+        tile(1, k)
+
+    def relayed(k):
+        for r in (3, 5):
+            landed(r, k)
+            tile(r, k)
+
+    def far(k):
+        tile(6, k)
+        landed(7, k)
+        tile(7, k)
+
+    incoming = {}
+    for k in range(1, npix):
+        for piece in range(PIECES):
+            part = rows(piece)
+            incoming[k, piece] = send(packed.at[k - 1, part], grid.at[0, k, part], at_pix(k))
+    stream = [(k, piece) for k in range(npix) for piece in range(PIECES)]
+    total_pieces = len(stream)
+
+    def begin(index):
+        if stream[index] in incoming:
+            incoming[stream[index]].wait_recv()
+        spread(*stream[index])
+
+    def finish(index):
+        k, piece = stream[index]
+        corner(k, piece)
+        if piece == PIECES - 1:
+            relayed(k)
+            far(k)
+
+    for index in range(LEAD):
+        begin(index)
+    for index, (k, piece) in enumerate(stream):
+        if index + LEAD < total_pieces:
+            begin(index + LEAD)
+        relay(k, piece)
+        if index >= LAG:
+            finish(index - LAG)
+        if piece == PIECES - 1:
+            near(k)
+    for index in range(total_pieces - LAG, total_pieces):
+        finish(index)
     for copy in copies:
         copy.wait_send()
 
@@ -170,25 +229,28 @@
 def fused(npix, frames, roi_ids, roi_order):
     fr, npx = frames.shape
     slot = SLOT
-    count = (npix - 1) + 9 * npix
-    vmem = pl.BlockSpec(memory_space=pltpu.VMEM)
+    count = (9 * npix - 1) * PIECES
     return pl.pallas_call(
         functools.partial(kernel, npix),
         out_shape=jax.ShapeDtypeStruct((1, fr, 8 * fr), F32),
-        in_specs=[pl.BlockSpec(memory_space=pltpu.SMEM), vmem, vmem],
-        out_specs=vmem,
+        in_specs=[pl.BlockSpec(memory_space=pltpu.HBM)] * 3,
+        out_specs=pl.BlockSpec(memory_space=pltpu.VMEM),
         scratch_shapes=[
+            pltpu.SMEM((npix,), jnp.int32),
+            pltpu.VMEM((1, npx), jnp.int32),
+            pltpu.VMEM((fr, npx), F32),
             pltpu.VMEM((npix - 1, slot, fr), F32),
             pltpu.VMEM((8, npix, slot, fr), F32),
             pltpu.VMEM((npix, fr, 3 * slot), BF16),
             pltpu.VMEM((8, 1, fr), F32),
+            pltpu.SemaphoreType.DMA((3,)),
             pltpu.SemaphoreType.DMA((count,)),
             pltpu.SemaphoreType.DMA((count,)),
         ],
         compiler_params=pltpu.CompilerParams(
             collective_id=0, has_side_effects=True, vmem_limit_bytes=40 * 1024 * 1024
         ),
-    )(roi_order, roi_ids, frames)
+    )(*(pltpu.with_memory_space_constraint(x, pltpu.HBM) for x in (roi_order, roi_ids.reshape(1, npx), frames)))
 
 
 def shifted(value, axis, steps):

time: 31.6 us -> 29.2 us (0.924)
  local copies, waits for them, and re-layouts: 3.73 us -> 1.32 us
    unnamed x6 -> x1, local copies, waits for them, and re-layouts: 3.73 us -> 1.32 us
where the time goes in v2:
time: 29.2 us; the launch traced here: 29.1 us
  Pallas kernels  27.7 us (95%)
  local copies, waits for them, and re-layouts  1.32 us (5%)
    pallas_call x1, Pallas kernels, fused(): pl.pallas_call(functools.partial(kernel, npix), out_shape=jax.ShapeDtypeS...  27.7 us
    unnamed x1, local copies, waits for them, and re-layouts  1.32 us

profile of v2, /device:TPU:0, one launch (start us, length us, event | category | flops | bytes accessed | tf_op | source)
XLA Modules:
  0.0 29.1 jit_solution(12399188560572110464)
XLA Ops:
  0.0 27.7 %shard_map.37 = f32[1,256,2048]{2,1,0:T(8,128)S(1)} custom-call(s32[4]{0:T(128)} %order_hbm.1, s32[1,256]{1,0:T(1,128)} %bitcast.1, f32[256,256]{1,0:T(8,128)} %frames_hbm.1), custom_call_target="tpu_custom_call" | custom-call | tf_op jit(solution)/shard_map/pallas_call | solution.py:233
  27.7 1.3 %copy.5 = f32[1,256,2048]{2,1,0:T(8,128)} copy(f32[1,256,2048]{2,1,0:T(8,128)S(1)} %shard_map.37) | data formatting | bytes 4194304
